TPU v7x, 512 devices: a whole 4x4x16 slice. The times are simulated.
512 devices in a mesh: level: 128 (over z, y_hi, x), sample: 4 (over y_lo, core).
Axes of the slice: x: 4, y: 4 (y_hi: 2, y_lo: 2; y = y_hi * 2 + y_lo), z: 16, core: 2. Of those that a mesh axis runs over, the one named last changes fastest.
Arguments:
- samples: bfloat16 [524288, 512], P('level', 'sample'), may hold values from -6 to 6
- sketch: bfloat16 [2, 128, 256], replicated, may hold values from -0.375 to 0.375
Outputs:
- far_factors: float32 [2048, 128, 128], P('level')
- near_factors: float32 [1024, 128, 128], P('level')
- basis_rows: float32 [131072, 512], P('level', 'sample')
All inputs are finite; a program needn't handle non-finite values.
Results may differ from a plain program's by a relative error of at most 0.0031.
Values may be sent and summed in bfloat16 or wider, within the bound.
No kernel may reach another device: no remote copies, remote signals or barrier semaphores. Data moves between devices by JAX's collectives and lax.ppermute only.
A program may use at most 64 MiB of HBM per device.

v0:
```python
import math

import jax
import jax.numpy as jnp
from jax import lax
from jax.sharding import PartitionSpec as P

SAMPLES = 512


def sent_to_all(value, axis):
    length = lax.axis_size(axis)
    return lax.all_to_all(
        jnp.broadcast_to(value[None], (length, *value.shape)), axis, 0, 0, tiled=True
    )


def taken_together(value, axis):
    everything = sent_to_all(value, axis)
    return jnp.sum(everything, axis=0)


def partner(value, axis, distance):
    mask = 2**distance
    pairs = [(source, source ^ mask) for source in range(lax.axis_size(axis))]
    return lax.ppermute(value, axis, pairs)


def split_half(rows, bit):
    count = rows.shape[0] // 2
    upper = lax.axis_index("level") // (1 << bit) % 2
    kept = lax.dynamic_slice_in_dim(rows, upper * count, count, 0)
    given = lax.dynamic_slice_in_dim(rows, (1 - upper) * count, count, 0)
    return (kept, given, upper)


def solve_box(factor_box, block_box):
    return jax.scipy.linalg.solve_triangular(factor_box, block_box, lower=True)


def batch_product(first, second):
    return jnp.einsum("brs,bst->brt", first, second, precision=lax.Precision.HIGHEST)


def factor_inverse(gram):
    order = gram.shape[1]
    if order <= 32:
        factor = jnp.linalg.cholesky(gram)
        eye_block = jnp.broadcast_to(jnp.eye(order, dtype=jnp.float32), gram.shape)
        inverse = jax.vmap(solve_box)(factor, eye_block)
        return (factor, inverse)
    middle = order // 2
    top_factor, top_inverse = factor_inverse(gram[:, :middle, :middle])
    lower_left = batch_product(gram[:, middle:, :middle], jnp.swapaxes(top_inverse, 1, 2))
    schur = gram[:, middle:, middle:] - batch_product(lower_left, jnp.swapaxes(lower_left, 1, 2))
    bottom_factor, bottom_inverse = factor_inverse(schur)
    inverse_left = -batch_product(batch_product(bottom_inverse, lower_left), top_inverse)
    zeros_block = jnp.zeros((gram.shape[0], middle, order - middle), jnp.float32)
    factor = jnp.concatenate(
        (
            jnp.concatenate((top_factor, zeros_block), axis=2),
            jnp.concatenate((lower_left, bottom_factor), axis=2),
        ),
        axis=1,
    )
    inverse = jnp.concatenate(
        (
            jnp.concatenate((top_inverse, zeros_block), axis=2),
            jnp.concatenate((inverse_left, bottom_inverse), axis=2),
        ),
        axis=1,
    )
    return (factor, inverse)


def quadrant_sum(partial_gram):
    boxes = partial_gram.shape[0]
    rank = partial_gram.shape[1]
    middle = rank // 2
    top_left = partial_gram[:, :middle, :middle]
    bottom_left = partial_gram[:, middle:, :middle]
    bottom_right = partial_gram[:, middle:, middle:]
    packed = jnp.stack((top_left, bottom_left, bottom_right), axis=1).reshape(
        boxes, 3 * middle * middle
    )
    summed = taken_together(packed, "sample").reshape(boxes, 3, middle, middle)
    top_left = summed[:, 0]
    bottom_left = summed[:, 1]
    bottom_right = summed[:, 2]
    top_half = jnp.concatenate((top_left, jnp.swapaxes(bottom_left, 1, 2)), axis=2)
    bottom_half = jnp.concatenate((bottom_left, bottom_right), axis=2)
    return jnp.concatenate((top_half, bottom_half), axis=1)


def compress(kept, received, upper, sketch_level):
    rank = sketch_level.shape[0]
    columns = kept.shape[1]
    boxes = kept.shape[0] // rank
    flag = upper == 1
    lower_rows = jnp.where(flag, received, kept).reshape(boxes, rank, columns)
    upper_rows = jnp.where(flag, kept, received).reshape(boxes, rank, columns)
    projected = jnp.einsum(
        "rm,bmc->brc", sketch_level[:, :rank], lower_rows, preferred_element_type=jnp.float32
    )
    projected = projected + jnp.einsum(
        "rm,bmc->brc", sketch_level[:, rank:], upper_rows, preferred_element_type=jnp.float32
    )
    partial_gram = jnp.einsum("brc,bsc->brs", projected, projected, precision=lax.Precision.HIGHEST)
    gram = quadrant_sum(partial_gram)
    factor, inverse = factor_inverse(gram)
    solved = jnp.einsum(
        "brs,bsc->brc", inverse, projected, precision=lax.Precision.HIGHEST
    ) * math.sqrt(SAMPLES)
    return (factor, solved.reshape(boxes * rank, columns))


def shards(samples, sketch):
    far_bit = lax.axis_size("level").bit_length() - 2
    kept, given, upper = split_half(samples, far_bit)
    received = partner(given, "level", far_bit)
    far_factors, first_rows = compress(kept, received, upper, sketch[0])
    first_rows = first_rows.astype(jnp.bfloat16)
    kept, given, upper = split_half(first_rows, 0)
    received = partner(given, "level", 0)
    near_factors, basis_rows = compress(kept, received, upper, sketch[1])
    return (far_factors, near_factors, basis_rows)


def solution(mesh):
    return jax.shard_map(
        shards,
        mesh=mesh,
        in_specs=(P("level", "sample"), P()),
        out_specs=(P("level", None, None), P("level", None, None), P("level", "sample")),
        check_vma=False,
    )
```

profile of v0, /device:TPU:39, one launch (start us, length us, event | category | flops | bytes accessed | tf_op | source)
XLA Modules:
  0.0 696.2 jit_solution(17540727460813259782)
XLA Ops:
  0.7 1.2 constant_dynamic-slice_fusion.1
  1.8 14.5 %collective-permute-start = (bf16[2048,128]{1,0:T(8,128)(2,1)S(1)}, bf16[2048,128]{1,0:T(8,128)(2,1)S(1)}, u32[]{:S(2)}, u32[]{:S(2)}) collective-permute-start(bf16[2048,128]{1,0:T(8,128)(2,1)S(1)} %constant_dynamic-slice_fusion.1), channel_id=1, source_target_pairs={{0,256},{4,260},{8,264},{12,268},{16,272},{20,276},{24,280},{28,28... | collective-permute-start | bytes 1572872 | tf_op jit(solution)/shard_map/ppermute | solution.py:26
  16.4 0.9 slice_bitcast_fusion.10
  17.3 44.5 %collective-permute-done = bf16[2048,128]{1,0:T(8,128)(2,1)S(1)} collective-permute-done((bf16[2048,128]{1,0:T(8,128)(2,1)S(1)}, bf16[2048,128]{1,0:T(8,128)(2,1)S(1)}, u32[]{:S(2)}, u32[]{:S(2)}) %collective-permute-start) | collective-permute-done | bytes 524320 | tf_op jit(solution)/shard_map/ppermute | solution.py:26
  62.7 1.8 fusion.96
  65.7 1.9 broadcast_in_dim.49
  67.6 5.2 all-to-all-start
  72.8 36.0 %all-to-all-done = f32[4,16,12288]{2,1,0:T(8,128)S(1)} async-done(((f32[4,16,12288]{2,1,0:T(8,128)}), f32[4,16,12288]{2,1,0:T(8,128)S(1)}, u32[]{:S(2)}, u32[]{:S(2)}) %all-to-all-start) | async-done | bytes 3145760 | tf_op jit(solution)/shard_map/all_to_all | solution.py:13
  108.8 1.1 reduce_sum.18
  110.0 1.8 reshape.51
  112.2 46.9 %custom-call.24 = f32[16,32,32]{2,1,0:T(8,128)S(1)} custom-call(f32[16,32,32]{2,1,0:T(8,128)S(1)} %fusion.58), custom_call_target="Cholesky" | custom-call | tf_op jit(solution)/shard_map/jit(cholesky)/cholesky | solution.py:48
  159.3 0.8 select_bitcast_fusion.3
  160.1 39.4 %custom-call.25 = f32[16,1,32,32]{2,3,1,0:T(8,128)S(1)} custom-call(f32[16,1,32,32]{3,2,1,0:T(8,128)S(1)} %get-tuple-element.21), custom_call_target="InvertDiagBlocksLowerTriangular" | custom-call | tf_op jit(solution)/shard_map/vmap(jit(_solve_triangular))/triangular_solve | solution.py:38
  199.5 0.6 fusion.56
  200.1 0.8 fusion.39
  201.6 46.9 %custom-call.26 = f32[16,32,32]{2,1,0:T(8,128)S(1)} custom-call(f32[16,32,32]{2,1,0:T(8,128)S(1)} %fusion.55), custom_call_target="Cholesky" | custom-call | tf_op jit(solution)/shard_map/jit(cholesky)/cholesky | solution.py:48
  248.7 0.8 select_bitcast_fusion.2
  249.5 39.4 %custom-call.27 = f32[16,1,32,32]{2,3,1,0:T(8,128)S(1)} custom-call(f32[16,1,32,32]{3,2,1,0:T(8,128)S(1)} %get-tuple-element.19), custom_call_target="InvertDiagBlocksLowerTriangular" | custom-call | tf_op jit(solution)/shard_map/vmap(jit(_solve_triangular))/triangular_solve | solution.py:38
  290.4 1.0 fusion.16
  291.6 1.0 convolution_subtract_fusion
  292.8 46.9 %custom-call.28 = f32[16,32,32]{2,1,0:T(8,128)S(1)} custom-call(f32[16,32,32]{2,1,0:T(8,128)S(1)} %fusion.52), custom_call_target="Cholesky" | custom-call | tf_op jit(solution)/shard_map/jit(cholesky)/cholesky | solution.py:48
  339.8 0.8 select_bitcast_fusion.1
  340.6 39.4 %custom-call.29 = f32[16,1,32,32]{2,3,1,0:T(8,128)S(1)} custom-call(f32[16,1,32,32]{3,2,1,0:T(8,128)S(1)} %get-tuple-element.17), custom_call_target="InvertDiagBlocksLowerTriangular" | custom-call | tf_op jit(solution)/shard_map/vmap(jit(_solve_triangular))/triangular_solve | solution.py:38
  380.6 0.8 fusion.37
  382.1 46.9 %custom-call.30 = f32[16,32,32]{2,1,0:T(8,128)S(1)} custom-call(f32[16,32,32]{2,1,0:T(8,128)S(1)} %fusion.49), custom_call_target="Cholesky" | custom-call | tf_op jit(solution)/shard_map/jit(cholesky)/cholesky | solution.py:48
  429.2 0.8 select_bitcast_fusion
  430.0 39.6 %custom-call.31 = f32[16,1,32,32]{2,3,1,0:T(8,128)S(1)} custom-call(f32[16,1,32,32]{3,2,1,0:T(8,128)S(1)} %get-tuple-element.15), custom_call_target="InvertDiagBlocksLowerTriangular" | custom-call | tf_op jit(solution)/shard_map/vmap(jit(_solve_triangular))/triangular_solve | solution.py:38
  471.0 0.7 fusion.19
  471.7 0.6 convolution_negate_fusion
  472.4 2.4 fusion
  474.8 2.5 collective-permute-start.1
  477.3 6.4 collective-permute-done.1
  484.3 1.0 fusion.99
  485.9 1.3 broadcast_in_dim.52
  487.1 5.4 all-to-all-start.1
  492.6 1.1 select_maximum_fusion.7
  493.7 2.3 fusion.3
  496.0 15.8 %all-to-all-done.1 = f32[4,8,12288]{2,1,0:T(8,128)S(1)} async-done(((f32[4,8,12288]{2,1,0:T(8,128)}), f32[4,8,12288]{2,1,0:T(8,128)S(1)}, u32[]{:S(2)}, u32[]{:S(2)}) %all-to-all-start.1) | async-done | bytes 1572896 | tf_op jit(solution)/shard_map/all_to_all | solution.py:13
  512.6 23.4 %custom-call.32 = f32[8,32,32]{2,1,0:T(8,128)S(1)} custom-call(f32[8,32,32]{2,1,0:T(8,128)S(1)} %fusion.74), custom_call_target="Cholesky" | custom-call | tf_op jit(solution)/shard_map/jit(cholesky)/cholesky | solution.py:48
  536.3 19.7 %custom-call.33 = f32[8,1,32,32]{2,3,1,0:T(8,128)S(1)} custom-call(f32[8,1,32,32]{3,2,1,0:T(8,128)S(1)} %get-tuple-element.13), custom_call_target="InvertDiagBlocksLowerTriangular" | custom-call | tf_op jit(solution)/shard_map/vmap(jit(_solve_triangular))/triangular_solve | solution.py:38
  557.3 23.4 %custom-call.34 = f32[8,32,32]{2,1,0:T(8,128)S(1)} custom-call(f32[8,32,32]{2,1,0:T(8,128)S(1)} %fusion.71), custom_call_target="Cholesky" | custom-call | tf_op jit(solution)/shard_map/jit(cholesky)/cholesky | solution.py:48
  581.0 19.7 %custom-call.35 = f32[8,1,32,32]{2,3,1,0:T(8,128)S(1)} custom-call(f32[8,1,32,32]{3,2,1,0:T(8,128)S(1)} %get-tuple-element.11), custom_call_target="InvertDiagBlocksLowerTriangular" | custom-call | tf_op jit(solution)/shard_map/vmap(jit(_solve_triangular))/triangular_solve | solution.py:38
  603.2 23.4 %custom-call.36 = f32[8,32,32]{2,1,0:T(8,128)S(1)} custom-call(f32[8,32,32]{2,1,0:T(8,128)S(1)} %fusion.68), custom_call_target="Cholesky" | custom-call | tf_op jit(solution)/shard_map/jit(cholesky)/cholesky | solution.py:48
  626.9 19.7 %custom-call.37 = f32[8,1,32,32]{2,3,1,0:T(8,128)S(1)} custom-call(f32[8,1,32,32]{3,2,1,0:T(8,128)S(1)} %get-tuple-element.9), custom_call_target="InvertDiagBlocksLowerTriangular" | custom-call | tf_op jit(solution)/shard_map/vmap(jit(_solve_triangular))/triangular_solve | solution.py:38
  647.9 23.4 %custom-call.38 = f32[8,32,32]{2,1,0:T(8,128)S(1)} custom-call(f32[8,32,32]{2,1,0:T(8,128)S(1)} %fusion.65), custom_call_target="Cholesky" | custom-call | tf_op jit(solution)/shard_map/jit(cholesky)/cholesky | solution.py:48
  671.6 19.7 %custom-call.39 = f32[8,1,32,32]{2,3,1,0:T(8,128)S(1)} custom-call(f32[8,1,32,32]{3,2,1,0:T(8,128)S(1)} %get-tuple-element.6), custom_call_target="InvertDiagBlocksLowerTriangular" | custom-call | tf_op jit(solution)/shard_map/vmap(jit(_solve_triangular))/triangular_solve | solution.py:38
  693.1 2.1 convolution_multiply_fusion.1
  695.3 1.0 fusion.15
  (104 shorter events, 18.2 us)
Async XLA Ops:
  0.6 61.2 %copy-start.3 = (bf16[4096,128]{1,0:T(8,128)(2,1)S(1)}, bf16[4096,128]{1,0:T(8,128)(2,1)}, u32[]{:S(2)}) copy-start(bf16[4096,128]{1,0:T(8,128)(2,1)} %param.8) | copy-start | bytes 3145732
  1.8 60.0 %collective-permute-start = (bf16[2048,128]{1,0:T(8,128)(2,1)S(1)}, bf16[2048,128]{1,0:T(8,128)(2,1)S(1)}, u32[]{:S(2)}, u32[]{:S(2)}) collective-permute-start(bf16[2048,128]{1,0:T(8,128)(2,1)S(1)} %constant_dynamic-slice_fusion.1), channel_id=1, source_target_pairs={{0,256},{4,260},{8,264},{12,268},{16,272},{20,276},{24,280},{28,28... | collective-permute-start | bytes 1572872 | tf_op jit(solution)/shard_map/ppermute | solution.py:26
  62.7 1.9 copy-start
  67.6 41.2 %all-to-all-start = ((f32[4,16,12288]{2,1,0:T(8,128)}), f32[4,16,12288]{2,1,0:T(8,128)S(1)}, u32[]{:S(2)}, u32[]{:S(2)}) async-start(f32[4,16,12288]{2,1,0:T(8,128)} %broadcast_in_dim.49), calls=%async_computation | async-start | bytes 6291456 | tf_op jit(solution)/shard_map/all_to_all | solution.py:13
  471.0 1.4 copy-start.1
  474.8 8.8 %collective-permute-start.1 = (bf16[1024,128]{1,0:T(8,128)(2,1)S(1)}, bf16[1024,128]{1,0:T(8,128)(2,1)S(1)}, u32[]{:S(2)}, u32[]{:S(2)}) collective-permute-start(bf16[1024,128]{1,0:T(8,128)(2,1)S(1)} %constant_dynamic-slice_fusion), channel_id=1, source_target_pairs={{0,4},{4,0},{8,12},{12,8},{16,20},{20,16},{24,28},{28,24},{32,36},... | collective-permute-start | bytes 786440 | tf_op jit(solution)/shard_map/ppermute | solution.py:26
  487.1 5.4 copy-start.2
  487.1 24.7 %all-to-all-start.1 = ((f32[4,8,12288]{2,1,0:T(8,128)}), f32[4,8,12288]{2,1,0:T(8,128)S(1)}, u32[]{:S(2)}, u32[]{:S(2)}) async-start(f32[4,8,12288]{2,1,0:T(8,128)} %broadcast_in_dim.52), calls=%async_computation.1 | async-start | bytes 3145728 | tf_op jit(solution)/shard_map/all_to_all | solution.py:13
where the time goes:
time: 697 us; the launch traced here: 696 us
  other arithmetic  530 us (76%)
  waiting for transfers between devices  103 us (15%)
  starting transfers between devices  27.6 us (4%)
  matrix products  24.4 us (4%)
  local copies, waits for them, and re-layouts  10.5 us (2%)
    another operation x25, other arithmetic, factor_inverse(): factor = jnp.linalg.cholesky(gram)  283 us
    another operation x16, other arithmetic, solve_box(): return jax.scipy.linalg.solve_triangular(factor_box, block_box, lower=True)  240 us
    all_to_all x2, waiting for transfers between devices, sent_to_all(): lax.all_to_all(jnp.broadcast_to(value[None], (length, *value.shape)), axi...  51.9 us
    ppermute x2, waiting for transfers between devices, partner(): return lax.ppermute(value, axis, pairs)  50.9 us
    ppermute x2, starting transfers between devices, partner(): return lax.ppermute(value, axis, pairs)  17 us
  transfers between devices with their start and end apart: 4, of which 4 were waited for; matrix products, arithmetic and copies ran while one was open for 1% of the time, Pallas kernels for 0%

commit v1 on v0

v1 whole, which is shorter than its diff:
```python
import functools
import math
import jax
import jax.numpy as jnp
from jax import lax
from jax.experimental import pallas as pl
from jax.experimental.pallas import tpu as pltpu
from jax.sharding import Mesh, PartitionSpec as P

RANK = 128
B = 16
F32 = jnp.float32
BF16 = jnp.bfloat16


def split3(x):
    h = x.astype(BF16)
    r = x - h.astype(F32)
    m = r.astype(BF16)
    l = (r - m.astype(F32)).astype(BF16)
    return h, m, l


def dot_nn(a, b):
    return lax.dot_general(a, b, (((1,), (0,)), ((), ())), preferred_element_type=F32)


def dot_nt(a, b):
    return lax.dot_general(a, b, (((1,), (1,)), ((), ())), preferred_element_type=F32)


def take_lanes(x, index):
    return jnp.take_along_axis(x, index, axis=1)


def leaf(rows, lane, sub):
    rows = list(rows)
    for k in range(B):
        half, at = divmod(k, 8)
        here = sub == at
        pivot = rows[k][half][at:at + 1, :]
        r = lax.rsqrt(pivot)
        u = [part * r for part in rows[k]]
        full = list(u)
        full[half] = jnp.where(here, r, u[half])
        rows[k] = full
        for i in range(k + 1, B):
            ui = u[i // 8][i % 8:i % 8 + 1, :]
            new = []
            for t in range(2):
                old = rows[i][t]
                if t == half:
                    old = jnp.where(here, 0.0, old)
                new.append(old - ui * full[t])
            rows[i] = new
    out = [rows[0][0], rows[0][1]]
    for i in range(1, B):
        sel = (lane % B) == i
        out = [jnp.where(sel, rows[i][t], out[t]) for t in range(2)]
    return out


def factor(f_refs, boxes):
    lane = lax.broadcasted_iota(jnp.int32, (8, RANK), 1)
    sub = lax.broadcasted_iota(jnp.int32, (8, RANK), 0)
    lane_big = lax.broadcasted_iota(jnp.int32, (RANK, RANK), 1)
    row_big = lax.broadcasted_iota(jnp.int32, (RANK, RANK), 0)
    seg = lane // B
    for p in range(RANK // B):
        lo = B * p
        cat = [None, None]
        for b in range(boxes):
            for t in range(2):
                tile = f_refs[b][lo + 8 * t:lo + 8 * t + 8, :]
                rep = take_lanes(tile, lo + lane % B)
                cat[t] = rep if b == 0 else jnp.where(seg % boxes == b, rep, cat[t])
        rows = []
        for i in range(B):
            idx = seg * B + i
            rows.append([take_lanes(cat[t], idx) for t in range(2)])
        out = leaf(rows, lane, sub)
        q_big = lane_big // B
        for b in range(boxes):
            idx = b * B + lane % B
            rep = [take_lanes(out[t], idx) for t in range(2)]
            full = jnp.concatenate(rep, axis=0)
            r16 = lax.broadcasted_iota(jnp.int32, (B, RANK), 0)
            l16 = lax.broadcasted_iota(jnp.int32, (B, RANK), 1)
            wt = jnp.where(r16 <= l16 % B, full, 0.0)
            old = f_refs[b][...]
            if p == RANK // B - 1 and p == 0:
                continue
            pieces = []
            if lo > 0:
                pieces.append(jnp.zeros((lo, RANK), F32))
            pieces.append(wt)
            if lo + B < RANK:
                pieces.append(jnp.zeros((RANK - lo - B, RANK), F32))
            t_full = jnp.concatenate(pieces, axis=0)
            th, tm, tl = split3(t_full)
            fh, fm, fl = split3(old)
            prod = dot_nn(jnp.concatenate([fh, fm], axis=1), jnp.concatenate([th, th], axis=0))
            prod += dot_nn(jnp.concatenate([fh, fm], axis=1), jnp.concatenate([tm, tm], axis=0))
            prod += dot_nn(jnp.concatenate([fh, fl], axis=1), jnp.concatenate([tl, th], axis=0))
            pieces = []
            if lo > 0:
                pieces.append(prod[:lo])
            pieces.append(wt)
            if lo + B < RANK:
                pieces.append(prod[lo + B:])
            panel = jnp.concatenate(pieces, axis=0)
            pieces[1 if lo > 0 else 0] = full
            shown = jnp.concatenate(pieces, axis=0)
            in_block = q_big == p
            base = jnp.where(in_block, shown, old)
            if p < RANK // B - 1:
                h, m, l = (v.astype(F32) for v in split3(panel))
                x = jnp.where((q_big == 0) | (q_big == 1) | (q_big == 3), h,
                              jnp.where((q_big == 2) | (q_big == 5), m,
                                        jnp.where(q_big == 4, l, 0.0))).astype(BF16)
                y = jnp.where((q_big == 0) | (q_big == 2) | (q_big == 4), h,
                              jnp.where((q_big == 1) | (q_big == 5), m,
                                        jnp.where(q_big == 3, l, 0.0)))
                y = jnp.where(row_big >= lo + B, y, 0.0).astype(BF16)
                own = (row_big >= lo) & (row_big < lo + B) & (q_big > p)
                base = jnp.where(own, 0.0, base) - dot_nt(x, y)
            f_refs[b][...] = base


def body(boxes, split_columns, x_ref, s_ref, q_ref, l_ref, z_ref, f_ref):
    s = s_ref[...]
    parts = 512 // RANK
    for b in range(boxes):
        for c in range(parts):
            if split_columns:
                both = jnp.concatenate([x_ref[0, c, b], x_ref[1, c, b]], axis=0)
            else:
                cols = slice(c * RANK, (c + 1) * RANK)
                both = jnp.concatenate([x_ref[0, b, :, cols], x_ref[1, b, :, cols]], axis=0)
            z_ref[b, :, c * RANK:(c + 1) * RANK] = dot_nn(s, both)
        h, m, l = split3(z_ref[b])
        hm = jnp.concatenate([h, m], axis=0)
        p1 = dot_nt(h, hm)
        p2 = dot_nt(m, hm)
        g = p1[:, :RANK] + ((p1[:, RANK:] + p2[:, :RANK]) + (dot_nt(l, h) + dot_nt(h, l)) + p2[:, RANK:])
        f_ref[b] = g
    factor([f_ref.at[b] for b in range(boxes)], boxes)
    row = lax.broadcasted_iota(jnp.int32, (RANK, RANK), 0)
    col = lax.broadcasted_iota(jnp.int32, (RANK, RANK), 1)
    for b in range(boxes):
        f = f_ref[b]
        l_ref[b] = jnp.where(row > col, f, jnp.where(row == col, 1.0 / f, 0.0)).astype(l_ref.dtype)
        w = jnp.where(row <= col, f, 0.0).T * math.sqrt(512)
        wh, wm, wl = split3(w)
        zh, zm, zl = split3(z_ref[b])
        q = dot_nn(jnp.concatenate([wh, wm], axis=1), jnp.concatenate([zh, zh], axis=0))
        q += dot_nn(wh, zm)
        if split_columns:
            q_ref[b] = q.astype(q_ref.dtype)
        else:
            for c in range(parts):
                q_ref[c, b] = q[:, c * RANK:(c + 1) * RANK].astype(q_ref.dtype)


def level1(x, s):
    boxes = x.shape[2]
    return pl.pallas_call(
        functools.partial(body, boxes, True),
        out_shape=(jax.ShapeDtypeStruct((boxes, RANK, 512), BF16),
                   jax.ShapeDtypeStruct((boxes, RANK, RANK), BF16)),
        in_specs=[pl.BlockSpec(memory_space=pltpu.VMEM)] * 2,
        out_specs=[pl.BlockSpec(memory_space=pltpu.VMEM)] * 2,
        scratch_shapes=[pltpu.VMEM((boxes, RANK, 512), F32), pltpu.VMEM((boxes, RANK, RANK), F32)],
        compiler_params=pltpu.CompilerParams(vmem_limit_bytes=48 << 20),
    )(x, s)


def level2(x, s, dt):
    boxes = x.shape[1]
    return pl.pallas_call(
        functools.partial(body, boxes, False),
        out_shape=(jax.ShapeDtypeStruct((4, boxes, RANK, RANK), dt),
                   jax.ShapeDtypeStruct((boxes, RANK, RANK), dt)),
        in_specs=[pl.BlockSpec(memory_space=pltpu.VMEM)] * 2,
        out_specs=[pl.BlockSpec(memory_space=pltpu.VMEM)] * 2,
        scratch_shapes=[pltpu.VMEM((boxes, RANK, 512), F32), pltpu.VMEM((boxes, RANK, RANK), F32)],
        compiler_params=pltpu.CompilerParams(vmem_limit_bytes=48 << 20),
    )(x, s)


def shards(samples, sketch):
    parts = lax.axis_size("sample")
    columns = samples.shape[1]
    boxes = samples.shape[0] // (4 * parts * RANK)
    x = samples.reshape(2, 2, parts, boxes, RANK, columns)
    x = jnp.swapaxes(x, 1, 2).reshape(2 * parts, 2 * boxes, RANK, columns)
    x = lax.all_to_all(x, ("hi", "sample"), 0, 0, tiled=True)
    first, far = level1(x.reshape(2, parts, 2 * boxes, RANK, columns), sketch[0])
    far = lax.all_gather(far, "sample")
    far = jnp.swapaxes(far.reshape(parts, 2, boxes, RANK, RANK), 0, 1)
    far = far.reshape(2 * parts * boxes, RANK, RANK).astype(F32)
    x = lax.all_to_all(first.reshape(2, boxes, RANK, -1), "lo", 0, 0, tiled=True)
    basis, near = level2(x, sketch[1], BF16)
    near = lax.all_gather(near, "sample", tiled=True).astype(F32)
    basis = lax.all_to_all(basis, "sample", 0, 0, tiled=True)
    basis = basis.reshape(parts * boxes * RANK, columns).astype(F32)
    return (far, near, basis)


def solution(mesh):
    level, parts = mesh.devices.shape
    cut = Mesh(mesh.devices.reshape(2, level // 4, 2, parts), ("hi", "mid", "lo", "sample"))
    rows = ("hi", "mid", "lo")
    return jax.shard_map(
        shards,
        mesh=cut,
        in_specs=(P(rows, "sample"), P()),
        out_specs=(P(rows, None, None), P(rows, None, None), P(rows, "sample")),
        check_vma=False,
    )
```

time: 697 us -> 125 us (0.18)
  other arithmetic: 530 us -> 1.76 us
  waiting for transfers between devices: 103 us -> 56 us
  matrix products: 24.4 us -> 0 us
  Pallas kernels: 0 us -> 23.9 us
  blocking collectives: 0 us -> 15.3 us
  local copies, waits for them, and re-layouts: 10.5 us -> 3.39 us
    another operation x43 -> x0, other arithmetic: 523 us -> none  [the longest x25 283 us: factor_inverse(): factor = jnp.linalg.cholesky(gram)]
    ppermute x2 -> x0, waiting for transfers between devices: 50.9 us -> none  [partner(): return lax.ppermute(value, axis, pairs)]
    pallas_call x0 -> x2, Pallas kernels: none -> 23.9 us  [the longest x1 14.2 us: level1(): pl.pallas_call(functools.partial(body, boxes, True), out_shape=(jax.Shape...]
    dot_general x32 -> x0, matrix products: 20.4 us -> none  [the longest x24 11.9 us: batch_product(): jnp.einsum('brs,bst->brt', first, second, precision=lax.Precision.HIGHEST)]
    ppermute x2 -> x0, starting transfers between devices: 17 us -> none  [partner(): return lax.ppermute(value, axis, pairs)]
    all_gather x0 -> x2, blocking collectives: none -> 15.3 us  [the longest x1 8.35 us: shards(): far = lax.all_gather(far, 'sample')]
    all_to_all x2 -> x3, starting transfers between devices: 10.6 us -> 23.6 us  [the longest x1 16 us: shards(): x = lax.all_to_all(x, ('hi', 'sample'), 0, 0, tiled=True)]
    all_to_all x2 -> x3, waiting for transfers between devices: 51.9 us -> 56 us  [the longest x1 56 us: shards(): x = lax.all_to_all(x, ('hi', 'sample'), 0, 0, tiled=True)]
  transfers between devices with their start and end apart: 4 -> 3, of which waited for: 4 -> 1; matrix products, arithmetic and copies ran while one was open for 1% -> 2% of each run, Pallas kernels for 0% -> 0%
where the time goes in v1:
time: 125 us
  waiting for transfers between devices  56 us (45%)
  Pallas kernels  23.9 us (19%)
  starting transfers between devices  23.6 us (19%)
  blocking collectives  15.3 us (12%)
  local copies, waits for them, and re-layouts  3.39 us (3%)
  other arithmetic  1.76 us (1%)
    all_to_all x1, waiting for transfers between devices, shards(): x = lax.all_to_all(x, ('hi', 'sample'), 0, 0, tiled=True)  56 us
    all_to_all x1, starting transfers between devices, shards(): x = lax.all_to_all(x, ('hi', 'sample'), 0, 0, tiled=True)  16 us
    pallas_call x1, Pallas kernels, level1(): pl.pallas_call(functools.partial(body, boxes, True), out_shape=(jax.Shape...  14.2 us
    pallas_call x1, Pallas kernels, level2(): pl.pallas_call(functools.partial(body, boxes, False), out_shape=(jax.Shap...  9.7 us
    all_gather x1, blocking collectives, shards(): far = lax.all_gather(far, 'sample')  8.35 us
    all_gather x1, blocking collectives, shards(): near = lax.all_gather(near, 'sample', tiled=True).astype(F32)  6.96 us
    all_to_all x1, starting transfers between devices, shards(): lax.all_to_all(first.reshape(2, boxes, RANK, -1), 'lo', 0, 0, tiled=True)  4.02 us
    all_to_all x1, starting transfers between devices, shards(): basis = lax.all_to_all(basis, 'sample', 0, 0, tiled=True)  3.54 us
  transfers between devices with their start and end apart: 3, of which 1 were waited for; matrix products, arithmetic and copies ran while one was open for 2% of the time, Pallas kernels for 0%

profile of v1, /device:TPU:39, one launch (start us, length us, event | category | flops | bytes accessed | tf_op | source)
XLA Modules:
  0.0 124.6 jit_solution(16695073499106322379)
XLA Ops:
  0.6 2.3 %copy.7 = bf16[2,4,2,2,128,128]{5,4,3,2,1,0:T(8,128)(2,1)} copy(bf16[2,4,2,2,128,128]{5,4,3,1,2,0:T(8,128)(2,1)} %bitcast.20) | data formatting | bytes 2097152 | tf_op jit(solution)/shard_map/transpose | solution.py:196
  2.9 0.0 copy-start
  2.9 16.0 %all-to-all-start = ((bf16[8,4,128,128]{3,2,1,0:T(8,128)(2,1)}), bf16[8,4,128,128]{3,2,1,0:T(8,128)(2,1)S(1)}, u32[]{:S(2)}, u32[]{:S(2)}) async-start(bf16[8,4,128,128]{3,2,1,0:T(8,128)(2,1)} %bitcast.2), calls=%async_computation | async-start | bytes 2097152 | tf_op jit(solution)/shard_map/all_to_all | solution.py:197
  18.9 0.0 copy-done
  19.0 56.0 %all-to-all-done = bf16[8,4,128,128]{3,2,1,0:T(8,128)(2,1)S(1)} async-done(((bf16[8,4,128,128]{3,2,1,0:T(8,128)(2,1)}), bf16[8,4,128,128]{3,2,1,0:T(8,128)(2,1)S(1)}, u32[]{:S(2)}, u32[]{:S(2)}) %all-to-all-start) | async-done | bytes 1048608 | tf_op jit(solution)/shard_map/all_to_all | solution.py:197
  75.0 14.2 %shard_map.49 = (bf16[4,128,512]{2,1,0:T(8,128)(2,1)}, bf16[4,128,128]{2,1,0:T(8,128)(2,1)S(1)}) custom-call(bf16[2,4,4,128,128]{4,3,2,1,0:T(8,128)(2,1)S(1)} %bitcast.18, bf16[128,256]{1,0:T(8,128)(2,1)S(1)} %get-tuple-element.12.s_ref), custom_call_target="tpu_custom_call" | custom-call | tf_op jit(solution)/shard_map/pallas_call | solution.py:167
  89.2 4.0 %all-to-all-start.1 = ((bf16[2,2,128,512]{3,2,1,0:T(8,128)(2,1)}), bf16[2,2,128,512]{3,2,1,0:T(8,128)(2,1)S(1)}, u32[]{:S(2)}, u32[]{:S(2)}) async-start(bf16[2,2,128,512]{3,2,1,0:T(8,128)(2,1)} %bitcast.8), calls=%async_computation.1 | async-start | bytes 1048576 | tf_op jit(solution)/shard_map/all_to_all | solution.py:202
  93.2 8.3 %all-gather = bf16[16,128,128]{2,1,0:T(8,128)(2,1)S(1)} all-gather(bf16[4,128,128]{2,1,0:T(8,128)(2,1)S(1)} %get-tuple-element.7), channel_id=2, replica_groups=mesh['hi'=2,'mid'=32,'lo'=2,'sample'=4] {'sample'}, dimensions={0}, use_global_device_ids=true | all-gather | bytes 655360 | tf_op jit(solution)/shard_map/all_gather | solution.py:199
  101.5 0.0 all-to-all-done.1.x_ref
  101.5 9.7 %shard_map.50 = (bf16[4,2,128,128]{3,2,1,0:T(8,128)(2,1)}, bf16[2,128,128]{2,1,0:T(8,128)(2,1)S(1)}) custom-call(bf16[2,2,128,512]{3,2,1,0:T(8,128)(2,1)S(1)} %all-to-all-done.1.x_ref, bf16[128,256]{1,0:T(8,128)(2,1)S(1)} %get-tuple-element.11.s_ref), custom_call_target="tpu_custom_call" | custom-call | tf_op jit(solution)/shard_map/pallas_call | solution.py:180
  111.2 3.5 %all-to-all-start.2 = ((bf16[4,2,128,128]{3,2,1,0:T(8,128)(2,1)}), bf16[4,2,128,128]{3,2,1,0:T(8,128)(2,1)S(1)}, u32[]{:S(2)}, u32[]{:S(2)}) async-start(bf16[4,2,128,128]{3,2,1,0:T(8,128)(2,1)} %get-tuple-element.10), calls=%async_computation.2 | async-start | bytes 524288 | tf_op jit(solution)/shard_map/all_to_all | solution.py:205
  114.8 0.1 convert_bitcast_fusion
  114.9 1.1 copy.8
  115.9 7.0 %all_gather.11 = bf16[8,128,128]{2,1,0:T(8,128)(2,1)S(1)} all-gather(bf16[2,128,128]{2,1,0:T(8,128)(2,1)S(1)} %get-tuple-element.9), channel_id=1, replica_groups=mesh['hi'=2,'mid'=32,'lo'=2,'sample'=4] {'sample'}, dimensions={0}, use_global_device_ids=true | all-gather | bytes 327680 | tf_op jit(solution)/shard_map/all_gather | solution.py:204
  122.9 0.8 convert_element_type.25
  123.7 0.0 all-to-all-done.2
  123.7 0.8 bitcast_convert_fusion
  (1 shorter events, 0.0 us)
Async XLA Ops:
  2.9 16.0 %copy-start = (bf16[2,128,256]{2,1,0:T(8,128)(2,1)S(1)}, bf16[2,128,256]{2,1,0:T(8,128)(2,1)}, u32[]{:S(2)}) copy-start(bf16[2,128,256]{2,1,0:T(8,128)(2,1)} %param.3) | copy-start | bytes 393220
  2.9 72.0 %all-to-all-start = ((bf16[8,4,128,128]{3,2,1,0:T(8,128)(2,1)}), bf16[8,4,128,128]{3,2,1,0:T(8,128)(2,1)S(1)}, u32[]{:S(2)}, u32[]{:S(2)}) async-start(bf16[8,4,128,128]{3,2,1,0:T(8,128)(2,1)} %bitcast.2), calls=%async_computation | async-start | bytes 2097152 | tf_op jit(solution)/shard_map/all_to_all | solution.py:197
  89.2 12.4 %all-to-all-start.1 = ((bf16[2,2,128,512]{3,2,1,0:T(8,128)(2,1)}), bf16[2,2,128,512]{3,2,1,0:T(8,128)(2,1)S(1)}, u32[]{:S(2)}, u32[]{:S(2)}) async-start(bf16[2,2,128,512]{3,2,1,0:T(8,128)(2,1)} %bitcast.8), calls=%async_computation.1 | async-start | bytes 1048576 | tf_op jit(solution)/shard_map/all_to_all | solution.py:202
  111.2 12.5 %all-to-all-start.2 = ((bf16[4,2,128,128]{3,2,1,0:T(8,128)(2,1)}), bf16[4,2,128,128]{3,2,1,0:T(8,128)(2,1)S(1)}, u32[]{:S(2)}, u32[]{:S(2)}) async-start(bf16[4,2,128,128]{3,2,1,0:T(8,128)(2,1)} %get-tuple-element.10), calls=%async_computation.2 | async-start | bytes 524288 | tf_op jit(solution)/shard_map/all_to_all | solution.py:205

commit v2 on v1

v2 whole, which is shorter than its diff:
```python
import functools
import math
import jax
import jax.numpy as jnp
from jax import lax
from jax.experimental import pallas as pl
from jax.experimental.pallas import tpu as pltpu
from jax.sharding import Mesh, PartitionSpec as P

RANK = 128
B = 32
EARLY = 2
FAR = 1
NEAR = 8_000_000_000
TURN = 1
F32 = jnp.float32
BF16 = jnp.bfloat16


def split3(x):
    h = x.astype(BF16)
    r = x - h.astype(F32)
    m = r.astype(BF16)
    l = (r - m.astype(F32)).astype(BF16)
    return h, m, l


def dot_nn(a, b):
    return lax.dot_general(a, b, (((1,), (0,)), ((), ())), preferred_element_type=F32)


def dot_nt(a, b):
    return lax.dot_general(a, b, (((1,), (1,)), ((), ())), preferred_element_type=F32)


def take_lanes(x, index):
    return jnp.take_along_axis(x, index, axis=1)


def leaf(rows, lane, sub):
    parts = B // 8
    scaled, full, low, out = [], [], [], None
    for i in range(B):
        mine, at = divmod(i, 8)
        here = sub == at
        row = []
        for g in range(parts):
            if g < mine:
                value = None
                for k in range(8 * g, i):
                    term = scaled[k][mine][at:at + 1, :] * (low[k] if k // 8 == g else full[k][g])
                    value = -term if value is None else value - term
            else:
                value = rows[i][g]
                for k in range(i):
                    if g == mine and k // 8 == g:
                        value = jnp.where(sub == k % 8, 0.0, value)
                    value = value - scaled[k][mine][at:at + 1, :] * full[k][g]
            row.append(value)
        r = lax.rsqrt(row[mine][at:at + 1, :])
        u = [part * r for part in row]
        scaled.append(u)
        done = list(u)
        done[mine] = jnp.where(here, r, u[mine])
        full.append(done)
        low.append(jnp.where(sub <= at, done[mine], 0.0))
        if i == 0:
            out = done
        else:
            chosen = (lane % B) == i
            out = [jnp.where(chosen, done[g], out[g]) for g in range(parts)]
    return out


def side(parts, q, order):
    h, m, l = (v.astype(F32) for v in parts)
    first = jnp.where((q == 0) | (q == order), h, m)
    second = jnp.where(q == 0, h if order == 1 else l, jnp.where(q == 1, l if order == 1 else h, 0.0))
    return jnp.concatenate([first.astype(BF16), second.astype(BF16)], axis=1)


def factor(f_refs, boxes):
    lane = lax.broadcasted_iota(jnp.int32, (8, RANK), 1)
    sub = lax.broadcasted_iota(jnp.int32, (8, RANK), 0)
    row_big = lax.broadcasted_iota(jnp.int32, (RANK, RANK), 0)
    lane_big = lax.broadcasted_iota(jnp.int32, (RANK, RANK), 1)
    row_block = lax.broadcasted_iota(jnp.int32, (B, RANK), 0)
    lane_block = lax.broadcasted_iota(jnp.int32, (B, RANK), 1)
    q_big, seg, parts = lane_big // B, lane // B, B // 8
    for p in range(RANK // B):
        lo = B * p
        cat = [None] * parts
        for b in range(boxes):
            for t in range(parts):
                tile = f_refs[b][lo + 8 * t:lo + 8 * t + 8, :]
                rep = take_lanes(tile, lo + lane % B)
                cat[t] = rep if b == 0 else jnp.where(seg % boxes == b, rep, cat[t])
        rows = []
        for i in range(B):
            rows.append([take_lanes(cat[t], seg * B + i) if t >= i // 8 else None for t in range(parts)])
        out = leaf(rows, lane, sub)
        for b in range(boxes):
            full = jnp.concatenate([take_lanes(out[t], b * B + lane % B) for t in range(parts)], axis=0)
            wt = jnp.where(row_block <= lane_block % B, full, 0.0)
            th, tm, tl = split3(wt)
            none = jnp.zeros((B, RANK), BF16)
            stack = jnp.concatenate([th, tm, th, tm, tl, th, none, none], axis=0)
            old = f_refs[b][...]
            wide = take_lanes(old, lo + lane_big % B)
            prod = dot_nn(side(split3(wide), q_big, 1), stack)
            above = [prod[:lo]] if lo else []
            below = [prod[lo + B:]] if lo + B < RANK else []
            base = jnp.where(q_big == p, jnp.concatenate(above + [full] + below, axis=0), old)
            if below:
                panel = jnp.concatenate(above + [wt] + below, axis=0)
                own = (row_big >= lo) & (row_big < lo + B) & (q_big > p)
                x = side(split3(panel), q_big, 1)
                y = side(split3(jnp.where(row_big >= lo + B, panel, 0.0)), q_big, 2)
                base = jnp.where(own, 0.0, base) - dot_nt(x, y)
            f_refs[b][...] = base


def project(boxes, pair, s_ref, z_ref, f_ref):
    s = s_ref[...]
    for b in range(boxes):
        for c in range(512 // RANK):
            z_ref[b, :, c * RANK:(c + 1) * RANK] = dot_nn(s, jnp.concatenate(pair(c, b), axis=0))
        h, m, l = split3(z_ref[b])
        hm = jnp.concatenate([h, m], axis=0)
        p1 = dot_nt(h, hm)
        p2 = dot_nt(m, hm)
        g = p1[:, :RANK] + ((p1[:, RANK:] + p2[:, :RANK]) + (dot_nt(l, h) + dot_nt(h, l)) + p2[:, RANK:])
        f_ref[b] = g
    factor([f_ref.at[b] for b in range(boxes)], boxes)


def results(b, z_ref, f_ref):
    row = lax.broadcasted_iota(jnp.int32, (RANK, RANK), 0)
    col = lax.broadcasted_iota(jnp.int32, (RANK, RANK), 1)
    f = f_ref[b]
    low = jnp.where(row > col, f, jnp.where(row == col, 1.0 / f, 0.0)).astype(BF16)
    w = jnp.where(row <= col, f, 0.0).T * math.sqrt(512)
    wh, wm, wl = split3(w)
    zh, zm, zl = split3(z_ref[b])
    q = dot_nn(jnp.concatenate([wh, wm], axis=1), jnp.concatenate([zh, zh], axis=0))
    q += dot_nn(wh, zm)
    return low, q.astype(BF16)


def far_body(boxes, early, here_ref, *refs):
    s_ref, given_ref, kept_ref, l_ref, z_ref, f_ref = refs[-6:]
    late = boxes - early

    def pair(c, b):
        received = refs[0][c, b] if b < early else refs[-7][c, b - early]
        return [here_ref[c, late + b], received]

    project(boxes, pair, s_ref, z_ref, f_ref)
    half = boxes // 2
    for b in range(boxes):
        low, q = results(b, z_ref, f_ref)
        for c in range(512 // RANK):
            l_ref[c, b] = low
        if b < half:
            given_ref[b] = q
        else:
            kept_ref[b - half] = q


def near_body(boxes, kept_ref, received_ref, s_ref, out_ref, z_ref, f_ref):
    def columns(c):
        return slice(c * RANK, (c + 1) * RANK)

    def pair(c, b):
        return [kept_ref[b, :, columns(c)], received_ref[b, :, columns(c)]]

    project(boxes, pair, s_ref, z_ref, f_ref)
    for b in range(boxes):
        low, q = results(b, z_ref, f_ref)
        for c in range(512 // RANK):
            out_ref[c, b] = q[:, columns(c)]
            out_ref[c, boxes + b] = low


VMEM = pl.BlockSpec(memory_space=pltpu.VMEM)


def call(body, boxes, shapes, operands, cost):
    return pl.pallas_call(
        body,
        out_shape=tuple(jax.ShapeDtypeStruct(shape, BF16) for shape in shapes),
        in_specs=[VMEM] * len(operands),
        out_specs=(VMEM,) * len(shapes),
        scratch_shapes=[pltpu.VMEM((boxes, RANK, 512), F32), pltpu.VMEM((boxes, RANK, RANK), F32)],
        cost_estimate=pl.CostEstimate(flops=cost, bytes_accessed=1 << 20, transcendentals=0),
        compiler_params=pltpu.CompilerParams(vmem_limit_bytes=40 << 20),
    )(*operands)


def turn_body(flag_ref, s_ref, first_ref, second_ref):
    for level, out_ref in enumerate((first_ref, second_ref)):
        s = s_ref[level]
        turned = jnp.concatenate([s[:, RANK:], s[:, :RANK]], axis=1)
        out_ref[...] = jnp.where(flag_ref[level] == 1, turned, s)


def turn(sketch, flags):
    shape = jax.ShapeDtypeStruct(sketch.shape[1:], sketch.dtype)
    return pl.pallas_call(
        turn_body,
        out_shape=(shape, shape),
        in_specs=[pl.BlockSpec(memory_space=pltpu.SMEM), VMEM],
        out_specs=(VMEM, VMEM),
        cost_estimate=pl.CostEstimate(flops=TURN, bytes_accessed=1 << 20, transcendentals=0),
    )(flags, sketch)


def flip(value, axis):
    return lax.ppermute(value, axis, [(0, 1), (1, 0)])


def shared(value):
    return lax.all_to_all(value, "sample", 0, 0, tiled=True)


def shards(samples, sketch):
    parts = lax.axis_size("sample")
    columns = samples.shape[1]
    quarter = samples.shape[0] // 4
    half = quarter // (parts * RANK)
    boxes = 2 * half
    up1, up2 = lax.axis_index("hi"), lax.axis_index("lo")

    def rows(side, part):
        taken = lax.dynamic_slice_in_dim(samples, (2 * side + part) * quarter, quarter, 0)
        return taken.reshape(parts, half, RANK, columns)

    given = jnp.concatenate([rows(1 - up1, 1 - up2), rows(1 - up1, up2)], axis=1)
    kept = jnp.concatenate([rows(up1, 1 - up2), rows(up1, up2)], axis=1)
    first = flip(given[:, :EARLY], "hi") if EARLY else None
    here = shared(jnp.concatenate([given[:, EARLY:], kept], axis=1))
    moved = [flip(here[:, :boxes - EARLY], "hi")] if EARLY < boxes else []
    if EARLY:
        moved.insert(0, shared(first))
    s1, s2 = turn(sketch, jnp.stack([up1, up2]).astype(jnp.int32))
    shape = (half, RANK, parts * columns)
    q_given, q_kept, far = call(
        functools.partial(far_body, boxes, EARLY), boxes, (shape, shape, (parts, boxes, RANK, RANK)), (here, *moved, s1), FAR)
    received = flip(q_given, "lo")
    far = shared(far)
    out = call(functools.partial(near_body, half), half, ((parts, boxes, RANK, RANK),), (q_kept, received, s2), NEAR)[0]
    out, far = lax.optimization_barrier((out, far))
    out = shared(out)
    basis = out[:, :half].reshape(parts * half * RANK, columns).astype(F32)
    near = out[:, half:].reshape(parts * half, RANK, RANK).astype(F32)
    l_given, l_kept = far[:, :half], far[:, half:]
    far = jnp.where(up2 == 1, jnp.stack([l_given, l_kept]), jnp.stack([l_kept, l_given])).astype(F32)
    return (far.reshape(2 * parts * half, RANK, RANK), near, basis)


def solution(mesh):
    level, parts = mesh.devices.shape
    cut = Mesh(mesh.devices.reshape(2, level // 4, 2, parts), ("hi", "mid", "lo", "sample"))
    rows = ("hi", "mid", "lo")
    return jax.shard_map(
        shards,
        mesh=cut,
        in_specs=(P(rows, "sample"), P()),
        out_specs=(P(rows, None, None), P(rows, None, None), P(rows, "sample")),
        check_vma=False,
    )
```

time: 125 us -> 109 us (0.87)
  the two profiles are of different devices: /device:TPU:39 before, /device:TPU:470 now
where the time goes in v2:
time: 109 us
  waiting for transfers between devices  57.4 us (53%)
  starting transfers between devices  27.6 us (25%)
  Pallas kernels  16.3 us (15%)
  other arithmetic  4.44 us (4%)
  local copies, waits for them, and re-layouts  2.21 us (2%)
    ppermute x3, waiting for transfers between devices, flip(): return lax.ppermute(value, axis, [(0, 1), (1, 0)])  39.9 us
    all_to_all x4, waiting for transfers between devices, shared(): return lax.all_to_all(value, 'sample', 0, 0, tiled=True)  17.6 us
    pallas_call x2, Pallas kernels, call(): pl.pallas_call(body, out_shape=tuple((jax.ShapeDtypeStruct(shape, BF16) f...  14.7 us
    all_to_all x4, starting transfers between devices, shared(): return lax.all_to_all(value, 'sample', 0, 0, tiled=True)  14 us
    ppermute x3, starting transfers between devices, flip(): return lax.ppermute(value, axis, [(0, 1), (1, 0)])  13.6 us
  transfers between devices with their start and end apart: 7, of which 5 were waited for; matrix products, arithmetic and copies ran while one was open for 2% of the time, Pallas kernels for 8%

profile of v2, /device:TPU:470, one launch (start us, length us, event | category | flops | bytes accessed | tf_op | source)
XLA Modules:
  0.0 108.7 jit_solution(13808255556759914053)
XLA Ops:
  0.6 1.3 %constant_dynamic-slice_fusion = (bf16[1024,128]{1,0:T(8,128)(2,1)S(1)}, bf16[1024,128]{1,0:T(8,128)(2,1)S(1)}, bf16[1024,128]{1,0:T(8,128)(2,1)S(1)}, bf16[1024,128]{1,0:T(8,128)(2,1)S(1)}) fusion(bf16[4096,128]{1,0:T(8,128)(2,1)} %param.2, s32[]{:T(128)S(6)} %select_n.26, s32[]{:T(128)S(6)} %select_n.24, s32[]{:T(128)S(6)} %select_n.23, s32[]{:T(128)S(6)} %select_n.25), kind=kLoop, calls=%fused_computation.7 | loop fusion | bytes 2097168 | tf_op jit(solution)/shard_map/dynamic_slice | solution.py:235
  1.9 1.0 pad_maximum_fusion
  2.9 3.5 %all-to-all-start = ((bf16[4,6,128,128]{3,2,1,0:T(8,128)(2,1)}), bf16[4,6,128,128]{3,2,1,0:T(8,128)(2,1)S(1)}, u32[]{:S(2)}, u32[]{:S(2)}) async-start(bf16[4,6,128,128]{3,2,1,0:T(8,128)(2,1)} %pad_maximum_fusion), calls=%async_computation | async-start | bytes 1572864 | tf_op jit(solution)/shard_map/all_to_all | solution.py:223
  6.4 5.4 %collective-permute-start = (bf16[4,2,128,128]{3,2,1,0:T(8,128)(2,1)S(1)}, bf16[4,2,128,128]{3,2,1,0:T(8,128)(2,1)}, u32[]{:S(2)}, u32[]{:S(2)}) collective-permute-start(bf16[4,2,128,128]{3,2,1,0:T(8,128)(2,1)S(1)} %bitcast.22), channel_id=1, source_target_pairs={{0,256},{256,0},{1,257},{257,1},{2,258},{258,2},{3,259},{259,3},{4... | collective-permute-start | bytes 786440 | tf_op jit(solution)/shard_map/ppermute | solution.py:219
  11.8 6.2 %all-to-all-done.here_ref = bf16[4,6,128,128]{3,2,1,0:T(8,128)(2,1)S(1)} async-done(((bf16[4,6,128,128]{3,2,1,0:T(8,128)(2,1)}), bf16[4,6,128,128]{3,2,1,0:T(8,128)(2,1)S(1)}, u32[]{:S(2)}, u32[]{:S(2)}) %all-to-all-start) | async-done | bytes 786464 | tf_op jit(solution)/shard_map/all_to_all | solution.py:223
  18.0 5.4 %collective-permute-start.1 = (bf16[4,2,128,128]{3,2,1,0:T(8,128)(2,1)S(1)}, bf16[4,2,128,128]{3,2,1,0:T(8,128)(2,1)S(1)}, u32[]{:S(2)}, u32[]{:S(2)}) collective-permute-start(bf16[4,2,128,128]{3,2,1,0:T(8,128)(2,1)S(1)} %slice.20), channel_id=1, source_target_pairs={{0,256},{256,0},{1,257},{257,1},{2,258},{258,2},{3,259},{259,3},{4... | collective-permute-start | bytes 786440 | tf_op jit(solution)/shard_map/ppermute | solution.py:219
  23.5 36.5 %collective-permute-done = bf16[4,2,128,128]{3,2,1,0:T(8,128)(2,1)} collective-permute-done((bf16[4,2,128,128]{3,2,1,0:T(8,128)(2,1)S(1)}, bf16[4,2,128,128]{3,2,1,0:T(8,128)(2,1)}, u32[]{:S(2)}, u32[]{:S(2)}) %collective-permute-start) | collective-permute-done | bytes 262176 | tf_op jit(solution)/shard_map/ppermute | solution.py:219
  60.0 3.4 %all-to-all-start.1 = ((bf16[4,2,128,128]{3,2,1,0:T(8,128)(2,1)}), bf16[4,2,128,128]{3,2,1,0:T(8,128)(2,1)S(1)}, u32[]{:S(2)}, u32[]{:S(2)}) async-start(bf16[4,2,128,128]{3,2,1,0:T(8,128)(2,1)} %collective-permute-done), calls=%async_computation.1 | async-start | bytes 524288 | tf_op jit(solution)/shard_map/all_to_all | solution.py:223
  63.4 0.6 pad_add_fusion.flag_ref
  64.0 1.6 %shard_map.49 = (bf16[128,256]{1,0:T(8,128)(2,1)}, bf16[128,256]{1,0:T(8,128)(2,1)}) custom-call(s32[2]{0:T(128)} %pad_add_fusion.flag_ref, bf16[2,128,256]{2,1,0:T(8,128)(2,1)} %s_ref.1), custom_call_target="tpu_custom_call" | custom-call | flops 1 | bytes 1048576 | tf_op jit(solution)/shard_map/pallas_call | solution.py:209
  65.5 3.8 %all-to-all-done.1.refs_0_ = bf16[4,2,128,128]{3,2,1,0:T(8,128)(2,1)S(1)} async-done(((bf16[4,2,128,128]{3,2,1,0:T(8,128)(2,1)}), bf16[4,2,128,128]{3,2,1,0:T(8,128)(2,1)S(1)}, u32[]{:S(2)}, u32[]{:S(2)}) %all-to-all-start.1) | async-done | bytes 262176 | tf_op jit(solution)/shard_map/all_to_all | solution.py:223
  69.4 0.0 collective-permute-done.1.refs_1_
  69.4 0.0 copy-start
  69.4 0.8 copy-done
  70.2 7.8 %shard_map.50 = (bf16[2,128,512]{2,1,0:T(8,128)(2,1)S(1)}, bf16[2,128,512]{2,1,0:T(8,128)(2,1)S(1)}, bf16[4,4,128,128]{3,2,1,0:T(8,128)(2,1)}) custom-call(bf16[4,6,128,128]{3,2,1,0:T(8,128)(2,1)S(1)} %all-to-all-done.here_ref, bf16[4,2,128,128]{3,2,1,0:T(8,128)(2,1)S(1)} %all-to-all-done.1.refs_0_, ...), custom_call_target="tpu_custom_call" | custom-call | flops 1 | bytes 1048576 | tf_op jit(solution)/shard_map/pallas_call | solution.py:189
  78.0 2.7 %collective-permute-start.2 = (bf16[2,128,512]{2,1,0:T(8,128)(2,1)S(1)}, bf16[2,128,512]{2,1,0:T(8,128)(2,1)S(1)}, u32[]{:S(2)}, u32[]{:S(2)}) collective-permute-start(bf16[2,128,512]{2,1,0:T(8,128)(2,1)S(1)} %get-tuple-element.12), channel_id=1, source_target_pairs={{0,4},{4,0},{1,5},{5,1},{2,6},{6,2},{3,7},{7,3},{8,12},{12,8},{9,1... | collective-permute-start | bytes 786440 | tf_op jit(solution)/shard_map/ppermute | solution.py:219
  80.7 0.0 copy-start.1
  80.7 3.6 %all-to-all-start.2 = ((bf16[4,4,128,128]{3,2,1,0:T(8,128)(2,1)}), bf16[4,4,128,128]{3,2,1,0:T(8,128)(2,1)S(1)}, u32[]{:S(2)}, u32[]{:S(2)}) async-start(bf16[4,4,128,128]{3,2,1,0:T(8,128)(2,1)} %get-tuple-element.14), calls=%async_computation.2 | async-start | bytes 1048576 | tf_op jit(solution)/shard_map/all_to_all | solution.py:223
  84.3 3.4 %collective-permute-done.2.received_ref = bf16[2,128,512]{2,1,0:T(8,128)(2,1)S(1)} collective-permute-done((bf16[2,128,512]{2,1,0:T(8,128)(2,1)S(1)}, bf16[2,128,512]{2,1,0:T(8,128)(2,1)S(1)}, u32[]{:S(2)}, u32[]{:S(2)}) %collective-permute-start.2) | collective-permute-done | bytes 262176 | tf_op jit(solution)/shard_map/ppermute | solution.py:219
  87.7 0.0 copy-done.1
  87.7 7.0 %shard_map.51 = bf16[4,4,128,128]{3,2,1,0:T(8,128)(2,1)} custom-call(bf16[2,128,512]{2,1,0:T(8,128)(2,1)S(1)} %get-tuple-element.11.kept_ref, bf16[2,128,512]{2,1,0:T(8,128)(2,1)S(1)} %collective-permute-done.2.received_ref, bf16[128,256]{1,0:T(8,128)(2,1)S(1)} %copy-done.1), custom_call_target="tpu_custom_call" | custom-call | flops 8000000000 | bytes 1048576 | tf_op jit(solution)/shard_map/pallas_call | solution.py:189
  94.7 0.0 all-to-all-done.2
  94.7 3.5 %all-to-all-start.3 = ((bf16[4,4,128,128]{3,2,1,0:T(8,128)(2,1)}), bf16[4,4,128,128]{3,2,1,0:T(8,128)(2,1)S(1)}, u32[]{:S(2)}, u32[]{:S(2)}) async-start(bf16[4,4,128,128]{3,2,1,0:T(8,128)(2,1)} %shard_map.51), calls=%async_computation.3 | async-start | bytes 1048576 | tf_op jit(solution)/shard_map/all_to_all | solution.py:223
  98.2 0.1 maximum_select_fusion
  98.3 1.1 %bitcast_convert_fusion = f32[16,128,128]{2,1,0:T(8,128)} fusion(bf16[2,4,2,128,128]{4,3,2,1,0:T(8,128)(2,1)S(1)} %maximum_select_fusion), kind=kLoop, calls=%fused_computation.2 | loop fusion | flops 262144 | bytes 1572864 | tf_op jit(solution)/shard_map/convert_element_type | solution.py:257
  99.4 7.6 %all-to-all-done.3 = bf16[4,4,128,128]{3,2,1,0:T(8,128)(2,1)S(1)} async-done(((bf16[4,4,128,128]{3,2,1,0:T(8,128)(2,1)}), bf16[4,4,128,128]{3,2,1,0:T(8,128)(2,1)S(1)}, u32[]{:S(2)}, u32[]{:S(2)}) %all-to-all-start.3) | async-done | bytes 524320 | tf_op jit(solution)/shard_map/all_to_all | solution.py:223
  107.0 0.8 bitcast_convert_fusion.1
  107.9 0.9 bitcast_convert_fusion.2
  (3 shorter events, 0.1 us)
Async XLA Ops:
  2.9 15.1 %all-to-all-start = ((bf16[4,6,128,128]{3,2,1,0:T(8,128)(2,1)}), bf16[4,6,128,128]{3,2,1,0:T(8,128)(2,1)S(1)}, u32[]{:S(2)}, u32[]{:S(2)}) async-start(bf16[4,6,128,128]{3,2,1,0:T(8,128)(2,1)} %pad_maximum_fusion), calls=%async_computation | async-start | bytes 1572864 | tf_op jit(solution)/shard_map/all_to_all | solution.py:223
  6.4 53.6 %collective-permute-start = (bf16[4,2,128,128]{3,2,1,0:T(8,128)(2,1)S(1)}, bf16[4,2,128,128]{3,2,1,0:T(8,128)(2,1)}, u32[]{:S(2)}, u32[]{:S(2)}) collective-permute-start(bf16[4,2,128,128]{3,2,1,0:T(8,128)(2,1)S(1)} %bitcast.22), channel_id=1, source_target_pairs={{0,256},{256,0},{1,257},{257,1},{2,258},{258,2},{3,259},{259,3},{4... | collective-permute-start | bytes 786440 | tf_op jit(solution)/shard_map/ppermute | solution.py:219
  18.0 51.3 %collective-permute-start.1 = (bf16[4,2,128,128]{3,2,1,0:T(8,128)(2,1)S(1)}, bf16[4,2,128,128]{3,2,1,0:T(8,128)(2,1)S(1)}, u32[]{:S(2)}, u32[]{:S(2)}) collective-permute-start(bf16[4,2,128,128]{3,2,1,0:T(8,128)(2,1)S(1)} %slice.20), channel_id=1, source_target_pairs={{0,256},{256,0},{1,257},{257,1},{2,258},{258,2},{3,259},{259,3},{4... | collective-permute-start | bytes 786440 | tf_op jit(solution)/shard_map/ppermute | solution.py:219
  60.0 9.4 %all-to-all-start.1 = ((bf16[4,2,128,128]{3,2,1,0:T(8,128)(2,1)}), bf16[4,2,128,128]{3,2,1,0:T(8,128)(2,1)S(1)}, u32[]{:S(2)}, u32[]{:S(2)}) async-start(bf16[4,2,128,128]{3,2,1,0:T(8,128)(2,1)} %collective-permute-done), calls=%async_computation.1 | async-start | bytes 524288 | tf_op jit(solution)/shard_map/all_to_all | solution.py:223
  69.4 0.8 copy-start
  78.0 9.7 %collective-permute-start.2 = (bf16[2,128,512]{2,1,0:T(8,128)(2,1)S(1)}, bf16[2,128,512]{2,1,0:T(8,128)(2,1)S(1)}, u32[]{:S(2)}, u32[]{:S(2)}) collective-permute-start(bf16[2,128,512]{2,1,0:T(8,128)(2,1)S(1)} %get-tuple-element.12), channel_id=1, source_target_pairs={{0,4},{4,0},{1,5},{5,1},{2,6},{6,2},{3,7},{7,3},{8,12},{12,8},{9,1... | collective-permute-start | bytes 786440 | tf_op jit(solution)/shard_map/ppermute | solution.py:219
  80.7 7.0 %copy-start.1 = (bf16[128,256]{1,0:T(8,128)(2,1)S(1)}, bf16[128,256]{1,0:T(8,128)(2,1)}, u32[]{:S(2)}) copy-start(bf16[128,256]{1,0:T(8,128)(2,1)} %get-tuple-element.13.s_ref) | copy-start | bytes 196612
  80.7 13.9 %all-to-all-start.2 = ((bf16[4,4,128,128]{3,2,1,0:T(8,128)(2,1)}), bf16[4,4,128,128]{3,2,1,0:T(8,128)(2,1)S(1)}, u32[]{:S(2)}, u32[]{:S(2)}) async-start(bf16[4,4,128,128]{3,2,1,0:T(8,128)(2,1)} %get-tuple-element.14), calls=%async_computation.2 | async-start | bytes 1048576 | tf_op jit(solution)/shard_map/all_to_all | solution.py:223
  94.7 12.3 %all-to-all-start.3 = ((bf16[4,4,128,128]{3,2,1,0:T(8,128)(2,1)}), bf16[4,4,128,128]{3,2,1,0:T(8,128)(2,1)S(1)}, u32[]{:S(2)}, u32[]{:S(2)}) async-start(bf16[4,4,128,128]{3,2,1,0:T(8,128)(2,1)} %shard_map.51), calls=%async_computation.3 | async-start | bytes 1048576 | tf_op jit(solution)/shard_map/all_to_all | solution.py:223

commit v3 on v2

--- a/solution.py
+++ b/solution.py
@@ -12,7 +12,6 @@
 EARLY = 2
 FAR = 1
 NEAR = 8_000_000_000
-TURN = 1
 F32 = jnp.float32
 BF16 = jnp.bfloat16
 
@@ -120,8 +119,9 @@
             f_refs[b][...] = base
 
 
-def project(boxes, pair, s_ref, z_ref, f_ref):
+def project(boxes, pair, flag_ref, s_ref, z_ref, f_ref):
     s = s_ref[...]
+    s = jnp.where(flag_ref[0] == 1, jnp.concatenate([s[:, RANK:], s[:, :RANK]], axis=1), s)
     for b in range(boxes):
         for c in range(512 // RANK):
             z_ref[b, :, c * RANK:(c + 1) * RANK] = dot_nn(s, jnp.concatenate(pair(c, b), axis=0))
@@ -148,14 +148,14 @@
 
 
 def far_body(boxes, early, here_ref, *refs):
-    s_ref, given_ref, kept_ref, l_ref, z_ref, f_ref = refs[-6:]
+    flag_ref, s_ref, given_ref, kept_ref, l_ref, z_ref, f_ref = refs[-7:]
     late = boxes - early
 
     def pair(c, b):
-        received = refs[0][c, b] if b < early else refs[-7][c, b - early]
+        received = refs[0][c, b] if b < early else refs[-8][c, b - early]
         return [here_ref[c, late + b], received]
 
-    project(boxes, pair, s_ref, z_ref, f_ref)
+    project(boxes, pair, flag_ref, s_ref, z_ref, f_ref)
     half = boxes // 2
     for b in range(boxes):
         low, q = results(b, z_ref, f_ref)
@@ -167,14 +167,14 @@
             kept_ref[b - half] = q
 
 
-def near_body(boxes, kept_ref, received_ref, s_ref, out_ref, z_ref, f_ref):
+def near_body(boxes, kept_ref, received_ref, flag_ref, s_ref, out_ref, z_ref, f_ref):
     def columns(c):
         return slice(c * RANK, (c + 1) * RANK)
 
     def pair(c, b):
         return [kept_ref[b, :, columns(c)], received_ref[b, :, columns(c)]]
 
-    project(boxes, pair, s_ref, z_ref, f_ref)
+    project(boxes, pair, flag_ref, s_ref, z_ref, f_ref)
     for b in range(boxes):
         low, q = results(b, z_ref, f_ref)
         for c in range(512 // RANK):
@@ -189,30 +189,12 @@
     return pl.pallas_call(
         body,
         out_shape=tuple(jax.ShapeDtypeStruct(shape, BF16) for shape in shapes),
-        in_specs=[VMEM] * len(operands),
+        in_specs=[VMEM] * (len(operands) - 2) + [pl.BlockSpec(memory_space=pltpu.SMEM), VMEM],
         out_specs=(VMEM,) * len(shapes),
         scratch_shapes=[pltpu.VMEM((boxes, RANK, 512), F32), pltpu.VMEM((boxes, RANK, RANK), F32)],
         cost_estimate=pl.CostEstimate(flops=cost, bytes_accessed=1 << 20, transcendentals=0),
         compiler_params=pltpu.CompilerParams(vmem_limit_bytes=40 << 20),
     )(*operands)
-
-
-def turn_body(flag_ref, s_ref, first_ref, second_ref):
-    for level, out_ref in enumerate((first_ref, second_ref)):
-        s = s_ref[level]
-        turned = jnp.concatenate([s[:, RANK:], s[:, :RANK]], axis=1)
-        out_ref[...] = jnp.where(flag_ref[level] == 1, turned, s)
-
-
-def turn(sketch, flags):
-    shape = jax.ShapeDtypeStruct(sketch.shape[1:], sketch.dtype)
-    return pl.pallas_call(
-        turn_body,
-        out_shape=(shape, shape),
-        in_specs=[pl.BlockSpec(memory_space=pltpu.SMEM), VMEM],
-        out_specs=(VMEM, VMEM),
-        cost_estimate=pl.CostEstimate(flops=TURN, bytes_accessed=1 << 20, transcendentals=0),
-    )(flags, sketch)
 
 
 def flip(value, axis):
@@ -242,13 +224,13 @@
     moved = [flip(here[:, :boxes - EARLY], "hi")] if EARLY < boxes else []
     if EARLY:
         moved.insert(0, shared(first))
-    s1, s2 = turn(sketch, jnp.stack([up1, up2]).astype(jnp.int32))
+    f1, f2 = up1.astype(jnp.int32)[None], up2.astype(jnp.int32)[None]
     shape = (half, RANK, parts * columns)
     q_given, q_kept, far = call(
-        functools.partial(far_body, boxes, EARLY), boxes, (shape, shape, (parts, boxes, RANK, RANK)), (here, *moved, s1), FAR)
+        functools.partial(far_body, boxes, EARLY), boxes, (shape, shape, (parts, boxes, RANK, RANK)), (here, *moved, f1, sketch[0]), FAR)
     received = flip(q_given, "lo")
     far = shared(far)
-    out = call(functools.partial(near_body, half), half, ((parts, boxes, RANK, RANK),), (q_kept, received, s2), NEAR)[0]
+    out = call(functools.partial(near_body, half), half, ((parts, boxes, RANK, RANK),), (q_kept, received, f2, sketch[1]), NEAR)[0]
     out, far = lax.optimization_barrier((out, far))
     out = shared(out)
     basis = out[:, :half].reshape(parts * half * RANK, columns).astype(F32)

time: 109 us -> 108 us (level)
  the two profiles are of different devices: /device:TPU:470 before, /device:TPU:452 now
where the time goes in v3:
time: 108 us
  waiting for transfers between devices  59.2 us (55%)
  starting transfers between devices  28 us (26%)
  Pallas kernels  14.7 us (14%)
  other arithmetic  3.86 us (4%)
  local copies, waits for them, and re-layouts  1.38 us (1%)
    ppermute x3, waiting for transfers between devices, flip(): return lax.ppermute(value, axis, [(0, 1), (1, 0)])  39.5 us
    all_to_all x4, waiting for transfers between devices, shared(): return lax.all_to_all(value, 'sample', 0, 0, tiled=True)  19.7 us
    pallas_call x2, Pallas kernels, call(): pl.pallas_call(body, out_shape=tuple((jax.ShapeDtypeStruct(shape, BF16) f...  14.7 us
    ppermute x3, starting transfers between devices, flip(): return lax.ppermute(value, axis, [(0, 1), (1, 0)])  14.1 us
    all_to_all x4, starting transfers between devices, shared(): return lax.all_to_all(value, 'sample', 0, 0, tiled=True)  13.9 us
  transfers between devices with their start and end apart: 7, of which 5 were waited for; matrix products, arithmetic and copies ran while one was open for 1% of the time, Pallas kernels for 6%

profile of v3, /device:TPU:452, one launch (start us, length us, event | category | flops | bytes accessed | tf_op | source)
XLA Modules:
  0.0 107.8 jit_solution(92333982045322366)
XLA Ops:
  0.6 1.3 %constant_dynamic-slice_fusion = (bf16[1024,128]{1,0:T(8,128)(2,1)S(1)}, bf16[1024,128]{1,0:T(8,128)(2,1)S(1)}, bf16[1024,128]{1,0:T(8,128)(2,1)S(1)}, bf16[1024,128]{1,0:T(8,128)(2,1)S(1)}) fusion(bf16[4096,128]{1,0:T(8,128)(2,1)} %param.2, s32[]{:T(128)S(6)} %select_n.26, s32[]{:T(128)S(6)} %select_n.24, s32[]{:T(128)S(6)} %select_n.23, s32[]{:T(128)S(6)} %select_n.25), kind=kLoop, calls=%fused_computation.9 | loop fusion | bytes 2097168 | tf_op jit(solution)/shard_map/dynamic_slice | solution.py:217
  1.9 1.0 pad_maximum_fusion
  2.9 3.5 %all-to-all-start = ((bf16[4,6,128,128]{3,2,1,0:T(8,128)(2,1)}), bf16[4,6,128,128]{3,2,1,0:T(8,128)(2,1)S(1)}, u32[]{:S(2)}, u32[]{:S(2)}) async-start(bf16[4,6,128,128]{3,2,1,0:T(8,128)(2,1)} %pad_maximum_fusion), calls=%async_computation | async-start | bytes 1572864 | tf_op jit(solution)/shard_map/all_to_all | solution.py:205
  6.4 5.4 %collective-permute-start = (bf16[4,2,128,128]{3,2,1,0:T(8,128)(2,1)S(1)}, bf16[4,2,128,128]{3,2,1,0:T(8,128)(2,1)}, u32[]{:S(2)}, u32[]{:S(2)}) collective-permute-start(bf16[4,2,128,128]{3,2,1,0:T(8,128)(2,1)S(1)} %bitcast.26), channel_id=1, source_target_pairs={{0,256},{256,0},{1,257},{257,1},{2,258},{258,2},{3,259},{259,3},{4... | collective-permute-start | bytes 786440 | tf_op jit(solution)/shard_map/ppermute | solution.py:201
  11.8 6.2 %all-to-all-done.here_ref = bf16[4,6,128,128]{3,2,1,0:T(8,128)(2,1)S(1)} async-done(((bf16[4,6,128,128]{3,2,1,0:T(8,128)(2,1)}), bf16[4,6,128,128]{3,2,1,0:T(8,128)(2,1)S(1)}, u32[]{:S(2)}, u32[]{:S(2)}) %all-to-all-start) | async-done | bytes 786464 | tf_op jit(solution)/shard_map/all_to_all | solution.py:205
  18.0 0.0 copy-start
  18.0 5.6 %collective-permute-start.1 = (bf16[4,2,128,128]{3,2,1,0:T(8,128)(2,1)S(1)}, bf16[4,2,128,128]{3,2,1,0:T(8,128)(2,1)S(1)}, u32[]{:S(2)}, u32[]{:S(2)}) collective-permute-start(bf16[4,2,128,128]{3,2,1,0:T(8,128)(2,1)S(1)} %slice.28), channel_id=1, source_target_pairs={{0,256},{256,0},{1,257},{257,1},{2,258},{258,2},{3,259},{259,3},{4... | collective-permute-start | bytes 786440 | tf_op jit(solution)/shard_map/ppermute | solution.py:201
  23.6 36.3 %collective-permute-done = bf16[4,2,128,128]{3,2,1,0:T(8,128)(2,1)} collective-permute-done((bf16[4,2,128,128]{3,2,1,0:T(8,128)(2,1)S(1)}, bf16[4,2,128,128]{3,2,1,0:T(8,128)(2,1)}, u32[]{:S(2)}, u32[]{:S(2)}) %collective-permute-start) | collective-permute-done | bytes 262176 | tf_op jit(solution)/shard_map/ppermute | solution.py:201
  60.0 3.4 %all-to-all-start.1 = ((bf16[4,2,128,128]{3,2,1,0:T(8,128)(2,1)}), bf16[4,2,128,128]{3,2,1,0:T(8,128)(2,1)S(1)}, u32[]{:S(2)}, u32[]{:S(2)}) async-start(bf16[4,2,128,128]{3,2,1,0:T(8,128)(2,1)} %collective-permute-done), calls=%async_computation.1 | async-start | bytes 524288 | tf_op jit(solution)/shard_map/all_to_all | solution.py:205
  63.4 0.0 copy-done
  63.4 6.0 %all-to-all-done.1.refs_0_ = bf16[4,2,128,128]{3,2,1,0:T(8,128)(2,1)S(1)} async-done(((bf16[4,2,128,128]{3,2,1,0:T(8,128)(2,1)}), bf16[4,2,128,128]{3,2,1,0:T(8,128)(2,1)S(1)}, u32[]{:S(2)}, u32[]{:S(2)}) %all-to-all-start.1) | async-done | bytes 262176 | tf_op jit(solution)/shard_map/all_to_all | solution.py:205
  69.4 0.0 collective-permute-done.1.refs_1_
  69.4 7.8 %shard_map.49 = (bf16[2,128,512]{2,1,0:T(8,128)(2,1)S(1)}, bf16[2,128,512]{2,1,0:T(8,128)(2,1)S(1)}, bf16[4,4,128,128]{3,2,1,0:T(8,128)(2,1)}) custom-call(bf16[4,6,128,128]{3,2,1,0:T(8,128)(2,1)S(1)} %all-to-all-done.here_ref, bf16[4,2,128,128]{3,2,1,0:T(8,128)(2,1)S(1)} %all-to-all-done.1.refs_0_, ...), custom_call_target="tpu_custom_call" | custom-call | flops 1 | bytes 1048576 | tf_op jit(solution)/shard_map/pallas_call | solution.py:189
  77.1 3.1 %collective-permute-start.2 = (bf16[2,128,512]{2,1,0:T(8,128)(2,1)S(1)}, bf16[2,128,512]{2,1,0:T(8,128)(2,1)S(1)}, u32[]{:S(2)}, u32[]{:S(2)}) collective-permute-start(bf16[2,128,512]{2,1,0:T(8,128)(2,1)S(1)} %get-tuple-element.9), channel_id=1, source_target_pairs={{0,4},{4,0},{1,5},{5,1},{2,6},{6,2},{3,7},{7,3},{8,12},{12,8},{9,1... | collective-permute-start | bytes 786440 | tf_op jit(solution)/shard_map/ppermute | solution.py:201
  80.2 3.5 %all-to-all-start.2 = ((bf16[4,4,128,128]{3,2,1,0:T(8,128)(2,1)}), bf16[4,4,128,128]{3,2,1,0:T(8,128)(2,1)S(1)}, u32[]{:S(2)}, u32[]{:S(2)}) async-start(bf16[4,4,128,128]{3,2,1,0:T(8,128)(2,1)} %get-tuple-element.10), calls=%async_computation.2 | async-start | bytes 1048576 | tf_op jit(solution)/shard_map/all_to_all | solution.py:205
  83.7 3.1 %collective-permute-done.2.received_ref = bf16[2,128,512]{2,1,0:T(8,128)(2,1)S(1)} collective-permute-done((bf16[2,128,512]{2,1,0:T(8,128)(2,1)S(1)}, bf16[2,128,512]{2,1,0:T(8,128)(2,1)S(1)}, u32[]{:S(2)}, u32[]{:S(2)}) %collective-permute-start.2) | collective-permute-done | bytes 262176 | tf_op jit(solution)/shard_map/ppermute | solution.py:201
  86.9 6.9 %shard_map.50 = bf16[4,4,128,128]{3,2,1,0:T(8,128)(2,1)} custom-call(bf16[2,128,512]{2,1,0:T(8,128)(2,1)S(1)} %get-tuple-element.8.kept_ref, bf16[2,128,512]{2,1,0:T(8,128)(2,1)S(1)} %collective-permute-done.2.received_ref, s32[1]{0:T(128)} %bitcast.6.flag_ref, bf16[128,256]{1,0:T(8,128)(2,1)S(1)} %get-tuple-element.21.s_ref), custom_call_target="tpu_custom_call" | custom-call | flops 8000000000 | bytes 1048576 | tf_op jit(solution)/shard_map/pallas_call | solution.py:189
  93.8 0.0 all-to-all-done.2
  93.8 3.5 %all-to-all-start.3 = ((bf16[4,4,128,128]{3,2,1,0:T(8,128)(2,1)}), bf16[4,4,128,128]{3,2,1,0:T(8,128)(2,1)S(1)}, u32[]{:S(2)}, u32[]{:S(2)}) async-start(bf16[4,4,128,128]{3,2,1,0:T(8,128)(2,1)} %shard_map.50), calls=%async_computation.3 | async-start | bytes 1048576 | tf_op jit(solution)/shard_map/all_to_all | solution.py:205
  97.3 0.1 maximum_select_fusion
  97.4 1.1 %bitcast_convert_fusion = f32[16,128,128]{2,1,0:T(8,128)} fusion(bf16[2,4,2,128,128]{4,3,2,1,0:T(8,128)(2,1)S(1)} %maximum_select_fusion), kind=kLoop, calls=%fused_computation.2 | loop fusion | flops 262144 | bytes 1572864 | tf_op jit(solution)/shard_map/convert_element_type | solution.py:239
  98.5 7.6 %all-to-all-done.3 = bf16[4,4,128,128]{3,2,1,0:T(8,128)(2,1)S(1)} async-done(((bf16[4,4,128,128]{3,2,1,0:T(8,128)(2,1)}), bf16[4,4,128,128]{3,2,1,0:T(8,128)(2,1)S(1)}, u32[]{:S(2)}, u32[]{:S(2)}) %all-to-all-start.3) | async-done | bytes 524320 | tf_op jit(solution)/shard_map/all_to_all | solution.py:205
  106.1 0.8 bitcast_convert_fusion.1
  107.0 0.9 bitcast_convert_fusion.2
  (4 shorter events, 0.1 us)
Async XLA Ops:
  2.9 15.1 %all-to-all-start = ((bf16[4,6,128,128]{3,2,1,0:T(8,128)(2,1)}), bf16[4,6,128,128]{3,2,1,0:T(8,128)(2,1)S(1)}, u32[]{:S(2)}, u32[]{:S(2)}) async-start(bf16[4,6,128,128]{3,2,1,0:T(8,128)(2,1)} %pad_maximum_fusion), calls=%async_computation | async-start | bytes 1572864 | tf_op jit(solution)/shard_map/all_to_all | solution.py:205
  6.4 53.6 %collective-permute-start = (bf16[4,2,128,128]{3,2,1,0:T(8,128)(2,1)S(1)}, bf16[4,2,128,128]{3,2,1,0:T(8,128)(2,1)}, u32[]{:S(2)}, u32[]{:S(2)}) collective-permute-start(bf16[4,2,128,128]{3,2,1,0:T(8,128)(2,1)S(1)} %bitcast.26), channel_id=1, source_target_pairs={{0,256},{256,0},{1,257},{257,1},{2,258},{258,2},{3,259},{259,3},{4... | collective-permute-start | bytes 786440 | tf_op jit(solution)/shard_map/ppermute | solution.py:201
  18.0 45.3 %copy-start = (bf16[2,128,256]{2,1,0:T(8,128)(2,1)S(1)}, bf16[2,128,256]{2,1,0:T(8,128)(2,1)}, u32[]{:S(2)}) copy-start(bf16[2,128,256]{2,1,0:T(8,128)(2,1)} %param.3) | copy-start | bytes 393220
  18.0 51.3 %collective-permute-start.1 = (bf16[4,2,128,128]{3,2,1,0:T(8,128)(2,1)S(1)}, bf16[4,2,128,128]{3,2,1,0:T(8,128)(2,1)S(1)}, u32[]{:S(2)}, u32[]{:S(2)}) collective-permute-start(bf16[4,2,128,128]{3,2,1,0:T(8,128)(2,1)S(1)} %slice.28), channel_id=1, source_target_pairs={{0,256},{256,0},{1,257},{257,1},{2,258},{258,2},{3,259},{259,3},{4... | collective-permute-start | bytes 786440 | tf_op jit(solution)/shard_map/ppermute | solution.py:201
  60.0 9.4 %all-to-all-start.1 = ((bf16[4,2,128,128]{3,2,1,0:T(8,128)(2,1)}), bf16[4,2,128,128]{3,2,1,0:T(8,128)(2,1)S(1)}, u32[]{:S(2)}, u32[]{:S(2)}) async-start(bf16[4,2,128,128]{3,2,1,0:T(8,128)(2,1)} %collective-permute-done), calls=%async_computation.1 | async-start | bytes 524288 | tf_op jit(solution)/shard_map/all_to_all | solution.py:205
  77.1 9.7 %collective-permute-start.2 = (bf16[2,128,512]{2,1,0:T(8,128)(2,1)S(1)}, bf16[2,128,512]{2,1,0:T(8,128)(2,1)S(1)}, u32[]{:S(2)}, u32[]{:S(2)}) collective-permute-start(bf16[2,128,512]{2,1,0:T(8,128)(2,1)S(1)} %get-tuple-element.9), channel_id=1, source_target_pairs={{0,4},{4,0},{1,5},{5,1},{2,6},{6,2},{3,7},{7,3},{8,12},{12,8},{9,1... | collective-permute-start | bytes 786440 | tf_op jit(solution)/shard_map/ppermute | solution.py:201
  80.2 13.6 %all-to-all-start.2 = ((bf16[4,4,128,128]{3,2,1,0:T(8,128)(2,1)}), bf16[4,4,128,128]{3,2,1,0:T(8,128)(2,1)S(1)}, u32[]{:S(2)}, u32[]{:S(2)}) async-start(bf16[4,4,128,128]{3,2,1,0:T(8,128)(2,1)} %get-tuple-element.10), calls=%async_computation.2 | async-start | bytes 1048576 | tf_op jit(solution)/shard_map/all_to_all | solution.py:205
  93.8 12.3 %all-to-all-start.3 = ((bf16[4,4,128,128]{3,2,1,0:T(8,128)(2,1)}), bf16[4,4,128,128]{3,2,1,0:T(8,128)(2,1)S(1)}, u32[]{:S(2)}, u32[]{:S(2)}) async-start(bf16[4,4,128,128]{3,2,1,0:T(8,128)(2,1)} %shard_map.50), calls=%async_computation.3 | async-start | bytes 1048576 | tf_op jit(solution)/shard_map/all_to_all | solution.py:205
